TPU v7x, 32 devices: a whole 2x2x4 slice. The times are simulated.
32 devices in a mesh: dp: 8 (over y, x, core), mp: 4 (over z).
Axes of the slice: x: 2, y: 2, z: 4, core: 2. Of those that a mesh axis runs over, the one named last changes fastest.
Arguments:
- gen_rows: bfloat16 [1024, 5120], P(('dp', 'mp')), may hold values from -6 to 6
- lengths: int32 [32, 4], P('dp'), may hold values from 1 to 16, 32 in all within a row
- assign: int32 [32, 4], P('dp'), may hold values from 0 to 3, each once within a row
- rewards: float32 [32, 4], P('dp'), may hold values from 0 to 1
- upstream: bfloat16 [2048, 2048], P('dp', 'mp'), may hold values from -6 to 6
- weight: bfloat16 [5120, 2048], P(None, 'mp'), may hold values from -0.078125 to 0.078125
- q_init: float32 [2048, 64], P('mp'), may hold values from -6 to 6
- resid: float32 [32, 128, 2048], P('dp', None, 'mp'), may hold values from -4 to 4
- block_ids: int32 [32], P('dp'), may hold values from 0 to 39, as said below
Outputs:
- p_factor: float32 [5120, 256], P(None, 'mp')
- q_factor: float32 [2048, 64], P('mp')
- resid_out: float32 [32, 128, 2048], P('dp', None, 'mp')
Inputs may be any that keep to these rules, and one draw needn't show every extreme that they name: Each row holds the lengths of one generator's 4 sequences; they sum to 32. `assign`: each row names every learner once. `block_ids`: the 4 ids of one replica are distinct.
All inputs are finite; a program needn't handle non-finite values.
Results may differ from a plain program's by a relative error of at most 0.003.
Values may be sent and summed in bfloat16 or wider, within the bound.
No kernel may reach another device: no remote copies, remote signals or barrier semaphores. Data moves between devices by JAX's collectives and lax.ppermute only.
A program may use at most 64 MiB of HBM per device.

v0:
```python
import jax
import jax.numpy as jnp
from jax import lax
from jax.sharding import PartitionSpec as P

HIGHEST_PRECISION = lax.Precision.HIGHEST


def packed_tables(lengths, assign, rewards, slot_count, capacity):
    groups, sequences = lengths.shape
    offsets = jnp.cumsum(lengths, axis=1) - lengths
    advantage = rewards - jnp.mean(rewards, axis=1, keepdims=True)
    seq_weight = advantage / lengths.astype(rewards.dtype)
    positions = jnp.arange(slot_count)
    seq_index = jnp.arange(sequences)
    inside = (offsets[:, None, :] <= positions[None, :, None]).astype(jnp.int32)
    owner = jnp.sum(inside, axis=2) - 1
    picked = owner[:, :, None] == seq_index[None, None, :]
    seq_start = jnp.sum(jnp.where(picked, offsets[:, None, :], 0), axis=2)
    learner = jnp.sum(jnp.where(picked, assign[:, None, :], 0), axis=2)
    row_weight = jnp.sum(jnp.where(picked, seq_weight[:, None, :], 0.0), axis=2)
    source = jnp.arange(groups)[:, None]
    slot_table = learner * (groups * capacity) + source * capacity + positions[None, :] - seq_start
    return (slot_table, row_weight)


def row_gradient(row_block, upstream_rows, weights_here, weight):
    hidden = jnp.dot(row_block, weight, preferred_element_type=jnp.float32)
    tangent = jnp.tanh(hidden)
    grad_h = (
        weights_here[:, None] * upstream_rows.astype(jnp.float32) * (1.0 - tangent * tangent)
    ).astype(jnp.bfloat16)
    return jnp.einsum("nd,nc->dc", row_block, grad_h, preferred_element_type=jnp.float32)


def shards(gen_rows, lengths, assign, rewards, upstream, weight, q_init, resid, block_ids):
    groups = lax.axis_size("mp")
    slot_count = gen_rows.shape[0]
    capacity = upstream.shape[0] // (groups * groups)
    slot_table, row_weight = packed_tables(lengths, assign, rewards, slot_count, capacity)
    flat_slot = slot_table.reshape(-1)
    flat_weight = row_weight.reshape(-1)
    upstream_rows = jnp.take(upstream, flat_slot, axis=0)
    gradient = row_gradient(
        lax.all_gather(gen_rows, "mp", axis=0, tiled=True), upstream_rows, flat_weight, weight
    )
    block_rows = resid.shape[1]
    for block in range(resid.shape[0]):
        first_row = block_ids[block] * block_rows
        current = lax.dynamic_slice_in_dim(gradient, first_row, block_rows, 0)
        gradient = lax.dynamic_update_slice_in_dim(gradient, current + resid[block], first_row, 0)
    p_local = jnp.dot(gradient, q_init, precision=HIGHEST_PRECISION)
    p_sum = lax.psum(p_local, "dp")
    gram_matrix = jnp.einsum("dr,ds->rs", p_sum, p_sum, precision=HIGHEST_PRECISION)
    factor_low = jnp.linalg.cholesky(gram_matrix)
    p_factor = jax.scipy.linalg.solve_triangular(factor_low, p_sum.T, lower=True).T
    q_local = jnp.einsum("dc,dr->cr", gradient, p_factor, precision=HIGHEST_PRECISION)
    q_factor = lax.psum(q_local, "dp") / lax.axis_size("dp")
    new_blocks = []
    for block in range(resid.shape[0]):
        first_row = block_ids[block] * block_rows
        merged_rows = lax.dynamic_slice_in_dim(gradient, first_row, block_rows, 0)
        p_rows = lax.dynamic_slice_in_dim(p_factor, first_row, block_rows, 0)
        approx = jnp.einsum("br,cr->bc", p_rows, q_factor, precision=HIGHEST_PRECISION)
        new_blocks.append(merged_rows - approx)
    return (p_factor, q_factor, jnp.stack(new_blocks))


def solution(mesh):
    placed = (
        P(("dp", "mp"), None),
        P("dp", None),
        P("dp", None),
        P("dp", None),
        P("dp", "mp"),
        P(None, "mp"),
        P("mp", None),
        P("dp", None, "mp"),
        P("dp"),
    )
    return jax.shard_map(
        shards,
        mesh=mesh,
        in_specs=placed,
        out_specs=(P(None, "mp"), P("mp", None), P("dp", None, "mp")),
        check_vma=False,
    )
```

profile of v0, /device:TPU:0, one launch (start us, length us, event | category | flops | bytes accessed | tf_op | source)
XLA Modules:
  0.0 227.9 jit_solution(15444329244682934595)
XLA Ops:
  7.2 0.7 all-gather.2.cloned.1.call-update
  8.0 0.9 reduce_window_sum.11
  8.8 0.7 sub.52
  9.6 0.8 select_reduce_fusion.2
  10.6 1.5 fusion.36
  14.8 0.8 reduce_sum.46
  15.6 0.8 convert_divide_fusion
  16.5 1.3 fusion.35
  17.9 0.1 copy.38
  18.4 0.8 gather_fusion
  19.2 25.8 %all-gather.2.cloned.1.call-done = bf16[128,5120]{1,0:T(8,128)(2,1)} async-done(((bf16[32,5120]{1,0:T(8,128)(2,1)}), bf16[128,5120]{1,0:T(8,128)(2,1)}) %all-gather.2.cloned.1.call-update) | async-done | bytes 1310736 | tf_op jit(solution)/shard_map/all_gather | solution.py:45
  45.0 9.6 %fusion.8 = f32[512,5120]{1,0:T(8,128)} fusion(bf16[128,5120]{1,0:T(8,128)(2,1)} %all-gather.2.cloned.1.call-done, bf16[5120,512]{1,0:T(8,128)(2,1)} %param.14, bf16[128,512]{1,0:T(8,128)(2,1)S(1)} %gather_fusion, f32[128]{0:T(128)S(1)} %mul.70, pred[128]{0:T(512)(128)(4,1)S(1)} %compare_and_fusion), kind=kOutput, calls=%fused_computation.14 | convolution fusion | flops 1342636032 | bytes 17171072 | tf_op jit(solution)/shard_map/nd,nc->dc/dot_general | solution.py:33
  54.6 4.0 %copy.40 = f32[5120,512]{0,1:T(8,128)S(1)} copy(f32[5120,512]{0,1:T(8,128)} %bitcast.57) | data formatting | bytes 20971520
  58.7 1.0 fusion.12
  59.9 4.0 %copy-done.1 = f32[5120,512]{0,1:T(8,128)} copy-done((f32[5120,512]{0,1:T(8,128)}, f32[5120,512]{0,1:T(8,128)S(1)}, u32[]{:S(2)}) %copy-start.1) | copy-done | bytes 10485784
  63.9 8.0 %fusion.37 = f32[5120,64]{0,1:T(8,128)} fusion(f32[5120,512]{0,1:T(8,128)S(1)} %fusion.9, f32[512,64]{0,1:T(8,128)S(1)} %copy-done.4), kind=kOutput, calls=%fused_computation.70 | convolution fusion | flops 2013265920 | bytes 11927552 | tf_op jit(solution)/shard_map/dot_general | solution.py:52
  72.0 0.2 all-reduce.5.cloned.1.call-start
  72.2 56.7 %all-reduce.3.cloned.1.call-done = f32[5120,64]{0,1:T(8,128)} async-done(((f32[5120,64]{0,1:T(8,128)}), f32[5120,64]{0,1:T(8,128)}) %all-reduce.3.cloned.1.call-update) | async-done | bytes 1310736 | tf_op jit(solution)/shard_map/psum | solution.py:53
  128.9 2.9 %fusion.38 = f32[64,64]{1,0:T(8,128)S(1)} fusion(f32[5120,64]{0,1:T(8,128)} %all-reduce.3.cloned.1.call-done), kind=kOutput, calls=%fused_computation.71 | convolution fusion | flops 251658240 | bytes 1327104 | tf_op jit(solution)/shard_map/dr,ds->rs/dot_general | solution.py:54
  131.9 5.8 %cholesky.16 = f32[64,64]{1,0:T(8,128)S(1)} custom-call(f32[64,64]{1,0:T(8,128)S(1)} %fusion.23), custom_call_target="Cholesky" | custom-call | tf_op jit(solution)/shard_map/jit(cholesky)/cholesky | solution.py:55
  137.7 0.6 compare_reduce_fusion
  138.4 0.7 fusion.20
  139.0 4.9 %custom-call.7 = f32[1,64,64]{1,2,0:T(8,128)S(1)} custom-call(f32[1,64,64]{2,1,0:T(8,128)S(1)} %fusion.20), custom_call_target="InvertDiagBlocksLowerTriangular" | custom-call | tf_op jit(solution)/shard_map/jit(_solve_triangular)/triangular_solve | solution.py:56
  143.9 2.6 %fusion.21 = f32[64,5120]{1,0:T(8,128)S(1)} fusion(f32[5120,64]{0,1:T(8,128)} %all-reduce.3.cloned.1.call-done, f32[1,64,64]{1,2,0:T(8,128)S(1)} %custom-call.7), kind=kOutput, calls=%fused_computation.34 | convolution fusion | flops 251658240 | bytes 2637824 | tf_op jit(solution)/shard_map/jit(_solve_triangular)/triangular_solve | solution.py:56
  146.5 13.9 %fusion.39 = f32[512,64]{0,1:T(8,128)} fusion(f32[5120,512]{0,1:T(8,128)} %copy-done.1, f32[64,5120]{1,0:T(8,128)S(1)} %fusion.21), kind=kOutput, calls=%fused_computation.72 | convolution fusion | flops 2013265920 | bytes 11927552 | tf_op jit(solution)/shard_map/dc,dr->cr/dot_general | solution.py:57
  160.5 52.3 %all-reduce.5.cloned.1.call-done = f32[512,64]{0,1:T(8,128)} async-done(((f32[512,64]{0,1:T(8,128)}), f32[512,64]{0,1:T(8,128)}) %all-reduce.5.cloned.1.call-update) | async-done | bytes 131088 | tf_op jit(solution)/shard_map/psum | solution.py:58
  212.7 0.9 broadcast_multiply_fusion
  213.7 1.6 fusion
  215.3 1.6 fusion.1
  216.8 1.6 fusion.2
  218.4 1.6 fusion.3
  220.1 1.3 copy.31
  (35 shorter events, 1.5 us)
Async XLA Ops:
  7.2 11.2 %copy-start = (bf16[256,512]{1,0:T(8,128)(2,1)S(1)}, bf16[256,512]{1,0:T(8,128)(2,1)}, u32[]{:S(2)}) copy-start(bf16[256,512]{1,0:T(8,128)(2,1)} %param.13) | copy-start | bytes 786436
  7.2 37.8 %all-gather.2.cloned.1.call-start = ((), (), s32[]{:S(2)}) async-start(), calls=%async_computation | async-start | bytes 1638400 | tf_op jit(solution)/shard_map/all_gather | solution.py:45
  7.9 120.9 %all-reduce.3.cloned.1.call-start = ((), (), s32[]{:S(2)}) async-start(), calls=%async_computation.1 | async-start | bytes 2621440 | tf_op jit(solution)/shard_map/psum | solution.py:53
  54.6 9.2 %copy-start.4 = (f32[512,64]{0,1:T(8,128)S(1)}, f32[512,64]{0,1:T(8,128)}, u32[]{:S(2)}) copy-start(f32[512,64]{0,1:T(8,128)} %param.15) | copy-start | bytes 393220
  59.9 4.0 %copy-start.1 = (f32[5120,512]{0,1:T(8,128)}, f32[5120,512]{0,1:T(8,128)S(1)}, u32[]{:S(2)}) copy-start(f32[5120,512]{0,1:T(8,128)S(1)} %fusion.9) | copy-start | bytes 31457284
  72.0 140.8 %all-reduce.5.cloned.1.call-start = ((), (), s32[]{:S(2)}) async-start(), calls=%async_computation.2 | async-start | bytes 262144 | tf_op jit(solution)/shard_map/psum | solution.py:58
  146.5 71.9 %copy-start.2 = (f32[64,5120]{1,0:T(8,128)}, f32[64,5120]{1,0:T(8,128)S(1)}, u32[]{:S(2)}) copy-start(f32[64,5120]{1,0:T(8,128)S(1)} %fusion.21) | copy-start | bytes 3932164
  213.7 7.7 %copy-start.3 = (f32[512,64]{0,1:T(8,128)}, f32[512,64]{0,1:T(8,128)S(1)}, u32[]{:S(2)}) copy-start(f32[512,64]{0,1:T(8,128)S(1)} %broadcast_multiply_fusion) | copy-start | bytes 393220
Sparse Core Ops, SparseCore 0:
  9.6 35.3 all-gather.1
  72.1 56.7 all-reduce.2
  160.6 52.1 all-reduce.4
where the time goes:
time: 228 us
  waiting for transfers between devices  135 us (59%)
  matrix products  43.3 us (19%)
  other arithmetic  18.4 us (8%)
  between operations  16.7 us (7%)
  local copies, waits for them, and re-layouts  13.7 us (6%)
    psum x1, waiting for transfers between devices, shards(): p_sum = lax.psum(p_local, 'dp')  56.7 us
    psum x1, waiting for transfers between devices, shards(): q_factor = lax.psum(q_local, 'dp') / lax.axis_size('dp')  52.3 us
    all_gather x1, waiting for transfers between devices, shards(): lax.all_gather(gen_rows, 'mp', axis=0, tiled=True)  25.8 us
    dot_general x1, matrix products, shards(): jnp.einsum('dc,dr->cr', gradient, p_factor, precision=HIGHEST_PRECISION)  13.9 us
    unnamed x16, local copies, waits for them, and re-layouts  9.83 us
    dot_general x1, matrix products, row_gradient(): jnp.einsum('nd,nc->dc', row_block, grad_h, preferred_element_type=jnp.flo...  9.64 us
    dot_general x1, matrix products, shards(): p_local = jnp.dot(gradient, q_init, precision=HIGHEST_PRECISION)  8.05 us
    another operation x3, other arithmetic, shards(): factor_low = jnp.linalg.cholesky(gram_matrix)  6.52 us
  transfers between devices with their start and end apart: 3, of which 3 were waited for; matrix products, arithmetic and copies ran while one was open for 4% of the time, Pallas kernels for 0%

commit v1 on v0

--- a/solution.py
+++ b/solution.py
@@ -50,7 +50,8 @@
         current = lax.dynamic_slice_in_dim(gradient, first_row, block_rows, 0)
         gradient = lax.dynamic_update_slice_in_dim(gradient, current + resid[block], first_row, 0)
     p_local = jnp.dot(gradient, q_init, precision=HIGHEST_PRECISION)
-    p_sum = lax.psum(p_local, "dp")
+    blocks = lax.all_gather(p_local, "dp", axis=0, tiled=False)
+    p_sum = blocks.sum(axis=0)
     gram_matrix = jnp.einsum("dr,ds->rs", p_sum, p_sum, precision=HIGHEST_PRECISION)
     factor_low = jnp.linalg.cholesky(gram_matrix)
     p_factor = jax.scipy.linalg.solve_triangular(factor_low, p_sum.T, lower=True).T

time: 228 us -> 245 us (1.075)
  local copies, waits for them, and re-layouts: 13.7 us -> 24 us
  waiting for transfers between devices: 135 us -> 142 us
  matrix products: 43.3 us -> 40.8 us
  other arithmetic: 18.4 us -> 20.9 us
    all_gather x0 -> x1, waiting for transfers between devices: none -> 62.2 us  [shards(): blocks = lax.all_gather(p_local, 'dp', axis=0, tiled=False)]
    psum x1 -> x0, waiting for transfers between devices: 56.7 us -> none  [shards(): p_sum = lax.psum(p_local, 'dp')]
    unnamed x16 -> x15, local copies, waits for them, and re-layouts: 9.83 us -> 20 us
    reduce_sum x0 -> x1, other arithmetic: none -> 2.46 us  [shards(): p_sum = blocks.sum(axis=0)]
  transfers between devices with their start and end apart: 3 -> 3, of which waited for: 3 -> 3; matrix products, arithmetic and copies ran while one was open for 4% -> 3% of each run, Pallas kernels for 0% -> 0%
where the time goes in v1:
time: 245 us; the launch traced here: 244 us
  waiting for transfers between devices  142 us (58%)
  matrix products  40.8 us (17%)
  local copies, waits for them, and re-layouts  24 us (10%)
  other arithmetic  20.9 us (9%)
  between operations  16.6 us (7%)
    all_gather x1, waiting for transfers between devices, shards(): blocks = lax.all_gather(p_local, 'dp', axis=0, tiled=False)  62.2 us
    psum x1, waiting for transfers between devices, shards(): q_factor = lax.psum(q_local, 'dp') / lax.axis_size('dp')  53.1 us
    all_gather x1, waiting for transfers between devices, shards(): lax.all_gather(gen_rows, 'mp', axis=0, tiled=True)  25.8 us
    unnamed x15, local copies, waits for them, and re-layouts  20 us
    dot_general x1, matrix products, shards(): jnp.einsum('dc,dr->cr', gradient, p_factor, precision=HIGHEST_PRECISION)  13 us
    dot_general x1, matrix products, row_gradient(): jnp.einsum('nd,nc->dc', row_block, grad_h, preferred_element_type=jnp.flo...  9.64 us
    dot_general x1, matrix products, shards(): p_local = jnp.dot(gradient, q_init, precision=HIGHEST_PRECISION)  8.05 us
    another operation x3, other arithmetic, shards(): factor_low = jnp.linalg.cholesky(gram_matrix)  6.52 us
  transfers between devices with their start and end apart: 3, of which 3 were waited for; matrix products, arithmetic and copies ran while one was open for 3% of the time, Pallas kernels for 0%

profile of v1, /device:TPU:0, one launch (start us, length us, event | category | flops | bytes accessed | tf_op | source)
XLA Modules:
  0.0 244.4 jit_solution(15489164073835107508)
XLA Ops:
  7.2 0.7 all-gather.4.cloned.1.call-update
  8.0 0.9 reduce_window_sum.11
  8.8 0.7 sub.52
  9.6 0.8 select_reduce_fusion.2
  10.6 1.5 fusion.36
  14.8 0.8 reduce_sum.55
  15.6 0.8 convert_divide_fusion
  16.5 1.3 fusion.35
  18.4 0.8 gather_fusion
  19.2 25.8 %all-gather.4.cloned.1.call-done = bf16[128,5120]{1,0:T(8,128)(2,1)} async-done(((bf16[32,5120]{1,0:T(8,128)(2,1)}), bf16[128,5120]{1,0:T(8,128)(2,1)}) %all-gather.4.cloned.1.call-update) | async-done | bytes 1310736 | tf_op jit(solution)/shard_map/all_gather | solution.py:45
  45.0 9.6 %fusion.8 = f32[512,5120]{1,0:T(8,128)} fusion(bf16[128,5120]{1,0:T(8,128)(2,1)} %all-gather.4.cloned.1.call-done, bf16[5120,512]{1,0:T(8,128)(2,1)} %param.14, bf16[128,512]{1,0:T(8,128)(2,1)S(1)} %gather_fusion, f32[128]{0:T(128)S(1)} %mul.70, pred[128]{0:T(512)(128)(4,1)S(1)} %compare_and_fusion), kind=kOutput, calls=%fused_computation.15 | convolution fusion | flops 1342636032 | bytes 17171072 | tf_op jit(solution)/shard_map/nd,nc->dc/dot_general | solution.py:33
  54.6 4.0 %copy.51 = f32[5120,512]{0,1:T(8,128)S(1)} copy(f32[5120,512]{0,1:T(8,128)} %bitcast.62) | data formatting | bytes 20971520
  58.7 1.0 fusion.12
  59.9 4.0 %copy-done.1 = f32[5120,512]{0,1:T(8,128)} copy-done((f32[5120,512]{0,1:T(8,128)}, f32[5120,512]{0,1:T(8,128)S(1)}, u32[]{:S(2)}) %copy-start.1) | copy-done | bytes 10485784
  63.9 8.0 %fusion.37 = f32[5120,64]{0,1:T(8,128)} fusion(f32[5120,512]{0,1:T(8,128)S(1)} %fusion.9, f32[512,64]{0,1:T(8,128)S(1)} %copy-done.3), kind=kOutput, calls=%fused_computation.71 | convolution fusion | flops 2013265920 | bytes 11927552 | tf_op jit(solution)/shard_map/dot_general | solution.py:52
  72.2 62.2 %all-gather.6.cloned.1.call-done = f32[40960,64]{0,1:T(8,128)} async-done(((f32[5120,64]{0,1:T(8,128)}), f32[40960,64]{0,1:T(8,128)}) %all-gather.6.cloned.1.call-update) | async-done | bytes 10485776 | tf_op jit(solution)/shard_map/all_gather | solution.py:53
  134.4 10.2 %copy.50 = f32[8,8,8,5120]{3,2,1,0:T(8,128)S(1)} copy(f32[8,8,8,5120]{3,1,2,0:T(8,128)} %bitcast.63) | data formatting | bytes 20971520
  144.6 2.5 %bitcast_reduce_fusion = f32[5120,64]{0,1:T(8,128)S(1)} fusion(f32[8,8,8,5120]{3,2,1,0:T(8,128)S(1)} %copy.50), kind=kLoop, calls=%fused_computation.1 | loop fusion | flops 2293760 | bytes 11796480 | tf_op jit(solution)/shard_map/reduce_sum | solution.py:54
  147.1 1.2 fusion.38
  148.3 5.8 %cholesky.16 = f32[64,64]{1,0:T(8,128)S(1)} custom-call(f32[64,64]{1,0:T(8,128)S(1)} %fusion.23), custom_call_target="Cholesky" | custom-call | tf_op jit(solution)/shard_map/jit(cholesky)/cholesky | solution.py:56
  154.2 0.6 compare_reduce_fusion
  154.9 0.7 fusion.20
  155.5 4.9 %custom-call.7 = f32[1,64,64]{1,2,0:T(8,128)S(1)} custom-call(f32[1,64,64]{2,1,0:T(8,128)S(1)} %fusion.20), custom_call_target="InvertDiagBlocksLowerTriangular" | custom-call | tf_op jit(solution)/shard_map/jit(_solve_triangular)/triangular_solve | solution.py:57
  160.4 2.6 %fusion.21 = f32[64,5120]{1,0:T(8,128)} fusion(f32[5120,64]{0,1:T(8,128)S(1)} %bitcast_reduce_fusion, f32[1,64,64]{1,2,0:T(8,128)S(1)} %custom-call.7), kind=kOutput, calls=%fused_computation.35 | convolution fusion | flops 251658240 | bytes 2637824 | tf_op jit(solution)/shard_map/jit(_solve_triangular)/triangular_solve | solution.py:57
  163.0 13.0 %fusion.39 = f32[512,64]{0,1:T(8,128)} fusion(f32[5120,512]{0,1:T(8,128)} %copy-done.1, f32[64,5120]{1,0:T(8,128)} %fusion.21), kind=kOutput, calls=%fused_computation.73 | convolution fusion | flops 2013265920 | bytes 11927552 | tf_op jit(solution)/shard_map/dc,dr->cr/dot_general | solution.py:58
  176.0 53.1 %all-reduce.2.cloned.1.call-done = f32[512,64]{0,1:T(8,128)} async-done(((f32[512,64]{0,1:T(8,128)}), f32[512,64]{0,1:T(8,128)}) %all-reduce.2.cloned.1.call-update) | async-done | bytes 131088 | tf_op jit(solution)/shard_map/psum | solution.py:59
  229.2 0.9 broadcast_multiply_fusion
  230.1 1.6 fusion
  231.7 1.6 fusion.1
  233.3 1.6 fusion.2
  234.9 1.6 fusion.3
  236.5 1.3 copy.41
  (35 shorter events, 1.8 us)
Async XLA Ops:
  7.2 11.2 %copy-start = (bf16[256,512]{1,0:T(8,128)(2,1)S(1)}, bf16[256,512]{1,0:T(8,128)(2,1)}, u32[]{:S(2)}) copy-start(bf16[256,512]{1,0:T(8,128)(2,1)} %param.13) | copy-start | bytes 786436
  7.2 37.8 %all-gather.4.cloned.1.call-start = ((), (), s32[]{:S(2)}) async-start(), calls=%async_computation | async-start | bytes 1638400 | tf_op jit(solution)/shard_map/all_gather | solution.py:45
  7.9 126.5 %all-gather.6.cloned.1.call-start = ((), (), s32[]{:S(2)}) async-start(), calls=%async_computation.2 | async-start | bytes 11796480 | tf_op jit(solution)/shard_map/all_gather | solution.py:53
  54.6 9.2 %copy-start.3 = (f32[512,64]{0,1:T(8,128)S(1)}, f32[512,64]{0,1:T(8,128)}, u32[]{:S(2)}) copy-start(f32[512,64]{0,1:T(8,128)} %param.15) | copy-start | bytes 393220
  59.9 4.0 %copy-start.1 = (f32[5120,512]{0,1:T(8,128)}, f32[5120,512]{0,1:T(8,128)S(1)}, u32[]{:S(2)}) copy-start(f32[5120,512]{0,1:T(8,128)S(1)} %fusion.9) | copy-start | bytes 31457284
  72.0 157.2 %all-reduce.2.cloned.1.call-start = ((), (), s32[]{:S(2)}) async-start(), calls=%async_computation.1 | async-start | bytes 262144 | tf_op jit(solution)/shard_map/psum | solution.py:59
  230.1 7.8 %copy-start.2 = (f32[512,64]{0,1:T(8,128)}, f32[512,64]{0,1:T(8,128)S(1)}, u32[]{:S(2)}) copy-start(f32[512,64]{0,1:T(8,128)S(1)} %broadcast_multiply_fusion) | copy-start | bytes 393220
Sparse Core Ops, SparseCore 0:
  9.6 35.3 all-gather.3
  72.1 62.2 all-gather.5
  176.2 52.9 all-reduce.1
